TPU v7x, 32 devices: a whole 2x2x4 slice. The times are simulated.
32 devices in a mesh: parts: 2 (over x), ctx: 16 (over z, y, core).
Axes of the slice: x: 2, y: 2, z: 4, core: 2. Of those that a mesh axis runs over, the one named last changes fastest.
Arguments:
- query_proj: bfloat16 [4096, 4096], P(('parts', 'ctx')), parts along dimension 0, may hold values from -6 to 6
- key_proj: bfloat16 [4096, 4096], P(('parts', 'ctx')), parts along dimension 0, may hold values from -6 to 6
- value_proj: bfloat16 [4096, 4096], P(('parts', 'ctx')), parts along dimension 0, may hold values from -6 to 6
- cotangent: bfloat16 [4096, 2048], P(('parts', 'ctx')), parts along dimension 0, may hold values from -6 to 6
- out_weight: bfloat16 [4096, 2048], P('ctx'), may hold values from -0.125 to 0.125
- filters: float32 [256, 2048], P('ctx'), may hold values from -1.2 to 1.2
Outputs:
- query_grad: float32 [4096, 4096], P(('parts', 'ctx')), parts along dimension 0
- key_grad: float32 [4096, 4096], P(('parts', 'ctx')), parts along dimension 0
- value_grad: float32 [4096, 4096], P(('parts', 'ctx')), parts along dimension 0
- filter_grad: float32 [512, 2048], P(('parts', 'ctx')), parts along dimension 0
There are 2 independent parts, one for each index of `parts`. A program takes and returns all parts, laid end to end along the dimension named above; an argument that names none is the same for every part. Nothing has to cross between parts.
All inputs are finite; a program needn't handle non-finite values.
Results may differ from a plain program's by a relative error of at most 0.005.
Values may be sent and summed in bfloat16 or wider, within the bound.
No kernel may reach another device: no remote copies, remote signals or barrier semaphores. Data moves between devices by JAX's collectives and lax.ppermute only.
A program may use at most 192 MiB of HBM per device.

v0:
```python
import math
import jax
import jax.numpy as jnp
from jax import lax
from jax.sharding import PartitionSpec as P

inner_len = 128


def dft_pair(size_count):
    index_row = jnp.arange(size_count, dtype=jnp.int32)
    phase = (index_row[:, None] * index_row[None, :] % size_count).astype(jnp.float32) * (
        -2.0 * math.pi / size_count
    )
    return (jnp.cos(phase), jnp.sin(phase))


def twist(spectrum, sign):
    outer_len = spectrum.shape[1]
    total = outer_len * inner_len
    outer_index = jnp.arange(outer_len, dtype=jnp.int32)[:, None, None]
    inner_index = jnp.arange(inner_len, dtype=jnp.int32)[None, None, :]
    phase = (outer_index * inner_index % total).astype(jnp.float32) * (-2.0 * math.pi / total)
    tw_real = jnp.cos(phase)
    tw_imag = jnp.sin(phase) * sign
    real_part = spectrum[0] * tw_real - spectrum[1] * tw_imag
    imag_part = spectrum[0] * tw_imag + spectrum[1] * tw_real
    return jnp.stack([real_part, imag_part])


def last_matrix(sign):
    last_real, last_imag = dft_pair(inner_len)
    last_imag = last_imag * sign
    return jnp.stack([jnp.stack([last_real, -last_imag]), jnp.stack([last_imag, last_real])])


def apply_last(spectrum, sign):
    return jnp.einsum(
        "qzcn,pqkn->pzck", spectrum, last_matrix(sign), precision=lax.Precision.HIGHEST
    )


def forward_spectrum(signal):
    half_rows = signal.shape[0]
    outer_len = 2 * half_rows
    lead_real, lead_imag = dft_pair(outer_len)
    lead = jnp.stack([lead_real[:, :half_rows], lead_imag[:, :half_rows]])
    spectrum = jnp.einsum("pzn,ncm->pzcm", lead, signal, precision=lax.Precision.HIGHEST)
    return apply_last(twist(spectrum, 1.0), 1.0)


def inverse_spectrum(spectrum, want_imag):
    outer_len = spectrum.shape[1]
    half_rows = outer_len // 2
    spectrum = twist(apply_last(spectrum, -1.0), -1.0)
    lead_real, lead_imag = dft_pair(outer_len)
    lead_real = lead_real[:half_rows]
    lead_imag = lead_imag[:half_rows]
    scale = 1.0 / (outer_len * inner_len)
    if want_imag:
        lead = jnp.stack([jnp.stack([lead_real, lead_imag]), jnp.stack([-lead_imag, lead_real])])
    else:
        lead = jnp.stack([lead_real, lead_imag])[None]
    return jnp.einsum("qzcm,pqtz->ptcm", spectrum, lead * scale, precision=lax.Precision.HIGHEST)


def to_blocks(array):
    seq_len, chans = array.shape
    return (
        array.astype(jnp.float32).reshape(seq_len // inner_len, inner_len, chans).transpose(0, 2, 1)
    )


def from_blocks(array):
    half_rows, chans, unused = array.shape
    return array.transpose(0, 2, 1).reshape(half_rows * inner_len, chans)


def channel_work(mixed, gated, filters):
    seq_len, chans = mixed.shape
    group_count = filters.shape[0]
    group_size = chans // group_count
    half_rows = seq_len // inner_len
    outer_len = 2 * half_rows
    split_shape = (2, outer_len, group_count, group_size, inner_len)
    mix_spec = forward_spectrum(to_blocks(mixed)).reshape(split_shape)
    gate_spec = forward_spectrum(to_blocks(gated)).reshape(split_shape)
    filter_blocks = filters.reshape(group_count, half_rows, inner_len).transpose(1, 0, 2)
    filt_spec = forward_spectrum(filter_blocks)[:, :, :, None, :]
    filt_real, filt_imag = (filt_spec[0], filt_spec[1])
    mix_real, mix_imag = (mix_spec[0], mix_spec[1])
    gate_real, gate_imag = (gate_spec[0], gate_spec[1])
    conv_real = filt_real * mix_real - filt_imag * mix_imag
    conv_imag = filt_real * mix_imag + filt_imag * mix_real
    corr_real = filt_real * gate_real + filt_imag * gate_imag
    corr_imag = filt_real * gate_imag - filt_imag * gate_real
    combined = jnp.stack([conv_real - corr_imag, conv_imag + corr_real]).reshape(
        2, outer_len, chans, inner_len
    )
    both = inverse_spectrum(combined, True)
    conv_out = from_blocks(both[0])
    mixed_grad = from_blocks(both[1])
    lag_real = jnp.sum(mix_real * gate_real + mix_imag * gate_imag, axis=2)
    lag_imag = jnp.sum(mix_real * gate_imag - mix_imag * gate_real, axis=2)
    lag_out = inverse_spectrum(jnp.stack([lag_real, lag_imag]), False)[0]
    filter_grad = lag_out.transpose(1, 0, 2).reshape(group_count, seq_len) * (
        group_size * seq_len
    ) ** (-0.5)
    return (conv_out, mixed_grad, filter_grad)


def rounded_product(left, right):
    product = (left.astype(jnp.float32) * right.astype(jnp.float32)).astype(jnp.bfloat16)
    return lax.optimization_barrier(product)


def per_device(query_proj, key_proj, value_proj, cotangent, out_weight, filters):
    grad_rows = jnp.einsum(
        "tj,cj->tc",
        cotangent,
        lax.all_gather(out_weight, "ctx", axis=0, tiled=True),
        preferred_element_type=jnp.float32,
    ).astype(jnp.bfloat16)
    query_cols, key_cols, value_cols, grad_cols = (
        lax.all_to_all(query_proj, "ctx", split_axis=1, concat_axis=0, tiled=True),
        lax.all_to_all(key_proj, "ctx", split_axis=1, concat_axis=0, tiled=True),
        lax.all_to_all(value_proj, "ctx", split_axis=1, concat_axis=0, tiled=True),
        lax.all_to_all(grad_rows, "ctx", split_axis=1, concat_axis=0, tiled=True),
    )
    mixed_cols = rounded_product(key_cols, value_cols)
    gated_cols = rounded_product(query_cols, grad_cols)
    conv_out, mixed_grad, filter_grad = channel_work(mixed_cols, gated_cols, filters)
    query_grad_cols = grad_cols.astype(jnp.float32) * conv_out
    query_grad, key_grad, value_grad = (
        lax.all_to_all(query_grad_cols, "ctx", split_axis=0, concat_axis=1, tiled=True),
        lax.all_to_all(
            mixed_grad * value_cols.astype(jnp.float32),
            "ctx",
            split_axis=0,
            concat_axis=1,
            tiled=True,
        ),
        lax.all_to_all(
            mixed_grad * key_cols.astype(jnp.float32),
            "ctx",
            split_axis=0,
            concat_axis=1,
            tiled=True,
        ),
    )
    return (query_grad, key_grad, value_grad, filter_grad)


def solution(mesh):
    placed = (
        P(("parts", "ctx"), None),
        P(("parts", "ctx"), None),
        P(("parts", "ctx"), None),
        P(("parts", "ctx"), None),
        P("ctx", None),
        P("ctx", None),
    )
    return jax.shard_map(
        per_device,
        mesh=mesh,
        in_specs=placed,
        out_specs=(
            P(("parts", "ctx"), None),
            P(("parts", "ctx"), None),
            P(("parts", "ctx"), None),
            P(("parts", "ctx"), None),
        ),
        check_vma=False,
    )
```

profile of v0, /device:TPU:13, one launch (start us, length us, event | category | flops | bytes accessed | tf_op | source)
XLA Modules:
  0.0 509.7 jit_solution(12436188474592288112)
XLA Ops:
  10.2 6.7 %all-to-all-start.1 = ((bf16[128,16,256]{0,2,1:T(8,128)(2,1)}), bf16[128,16,256]{0,2,1:T(8,128)(2,1)S(1)}, u32[]{:S(2)}, u32[]{:S(2)}) async-start(bf16[128,16,256]{0,2,1:T(8,128)(2,1)} %bitcast.30), calls=%async_computation.1 | async-start | bytes 2097152 | tf_op jit(solution)/shard_map/all_to_all | solution.py:126
  18.2 49.8 %all-to-all-done.1 = bf16[128,16,256]{0,2,1:T(8,128)(2,1)S(1)} async-done(((bf16[128,16,256]{0,2,1:T(8,128)(2,1)}), bf16[128,16,256]{0,2,1:T(8,128)(2,1)S(1)}, u32[]{:S(2)}, u32[]{:S(2)}) %all-to-all-start.1) | async-done | bytes 1048608 | tf_op jit(solution)/shard_map/all_to_all | solution.py:126
  74.2 46.1 %all-to-all-done.2 = bf16[128,16,256]{0,2,1:T(8,128)(2,1)S(1)} async-done(((bf16[128,16,256]{0,2,1:T(8,128)(2,1)}), bf16[128,16,256]{0,2,1:T(8,128)(2,1)S(1)}, u32[]{:S(2)}, u32[]{:S(2)}) %all-to-all-start.2) | async-done | bytes 1048608 | tf_op jit(solution)/shard_map/all_to_all | solution.py:127
  120.3 7.1 %all-to-all-start.3 = ((bf16[128,16,256]{0,2,1:T(8,128)(2,1)}), bf16[128,16,256]{0,2,1:T(8,128)(2,1)}, u32[]{:S(2)}, u32[]{:S(2)}) async-start(bf16[128,16,256]{0,2,1:T(8,128)(2,1)} %bitcast.223), calls=%async_computation.3 | async-start | bytes 2097152 | tf_op jit(solution)/shard_map/all_to_all | solution.py:125
  129.2 57.2 %all-gather.2.cloned.1.call-done = bf16[4096,2048]{1,0:T(8,128)(2,1)} async-done(((bf16[256,2048]{1,0:T(8,128)(2,1)}), bf16[4096,2048]{1,0:T(8,128)(2,1)}) %all-gather.2.cloned.1.call-update) | async-done | bytes 16777232 | tf_op jit(solution)/shard_map/all_gather | solution.py:121
  186.4 12.4 %convolution_convert_fusion = bf16[128,4096]{1,0:T(8,128)(2,1)} fusion(bf16[128,2048]{1,0:T(8,128)(2,1)S(1)} %copy-done, bf16[4096,2048]{1,0:T(8,128)(2,1)} %all-gather.2.cloned.1.call-done), kind=kOutput, calls=%fused_computation.13 | convolution fusion | flops 2148007936 | bytes 18350080 | tf_op jit(solution)/shard_map/tj,cj->tc/dot_general | solution.py:118
  201.0 10.4 %all-to-all-start = ((bf16[128,16,256]{0,2,1:T(8,128)(2,1)}), bf16[128,16,256]{0,2,1:T(8,128)(2,1)}, u32[]{:S(2)}, u32[]{:S(2)}) async-start(bf16[128,16,256]{0,2,1:T(8,128)(2,1)} %bitcast.222), calls=%async_computation | async-start | bytes 2097152 | tf_op jit(solution)/shard_map/all_to_all | solution.py:128
  215.2 5.7 %copy.104 = f32[1,32,256,128]{2,3,1,0:T(8,128)} copy(f32[1,32,256,128]{3,2,1,0:T(8,128)} %bitcast.214) | data formatting | bytes 8388608 | tf_op jit(solution)/shard_map/mul | solution.py:93
  223.4 5.6 %copy.106 = f32[1,32,256,128]{2,3,1,0:T(8,128)} copy(f32[1,32,256,128]{3,2,1,0:T(8,128)} %bitcast.215) | data formatting | bytes 8388608 | tf_op jit(solution)/shard_map/mul | solution.py:93
  230.8 5.6 %fusion.26 = f32[2,32,256,128]{3,1,2,0:T(8,128)} fusion(bf16[16,128,256]{1,0,2:T(8,128)(2,1)S(1)} %bitcast.218, f32[1,32,16]{2,1,0:T(8,128)S(1)} %get-tuple-element.47, f32[1,32,16]{2,1,0:T(8,128)S(1)} %get-tuple-element.48), kind=kOutput, calls=%fused_computation.48 | convolution fusion | flops 402654208 | bytes 9441280 | tf_op jit(solution)/shard_map/pzn,ncm->pzcm/dot_general | solution.py:48
  243.1 6.2 %multiply_subtract_fusion.3 = (f32[1,32,256,128]{3,1,2,0:T(8,128)}, f32[1,32,256,128]{3,1,2,0:T(8,128)}, f32[1,32,256,128]{3,1,2,0:T(8,128)S(1)}, f32[1,32,256,128]{3,1,2,0:T(8,128)}) fusion(f32[2,32,256,128]{3,1,2,0:T(8,128)S(1)} %bitcast.212, f32[32,128]{1,0:T(8,128)S(1)} %get-tuple-element.49, f32[32,128]{1,0:T(8,128)S(1)} %get-tuple-element.50, ...), kind=kLoop, calls=%fused_computation.23 | loop fusion | flops 12582912 | bytes 33587200 | tf_op jit(solution)/shard_map/sub | solution.py:26
  253.9 12.6 %fusion.9 = f32[2,32,256,128]{2,3,1,0:T(8,128)S(1)} fusion(f32[2,32,256,128]{3,1,2,0:T(8,128)S(1)} %pad_maximum_fusion, f32[1,2,128,128]{3,2,1,0:T(8,128)S(1)} %copy-done.6, f32[1,2,128,128]{3,2,1,0:T(8,128)S(1)} %copy-done.8), kind=kOutput, calls=%fused_computation.24 | convolution fusion | flops 6442516480 | bytes 17039360 | tf_op jit(solution)/shard_map/qzcn,pqkn->pzck/dot_general | solution.py:38
  269.7 16.7 %fusion.12 = f32[2,32,256,128]{2,3,1,0:T(8,128)} fusion(f32[2,32,256,128]{3,1,2,0:T(8,128)S(1)} %pad_maximum_fusion.1, f32[1,2,128,128]{3,2,1,0:T(8,128)S(1)} %copy-done.6, f32[1,2,128,128]{3,2,1,0:T(8,128)S(1)} %copy-done.8), kind=kOutput, calls=%fused_computation.25 | convolution fusion | flops 6442516480 | bytes 17039360 | tf_op jit(solution)/shard_map/qzcn,pqkn->pzck/dot_general | solution.py:38
  286.4 10.2 %multiply_add_fusion = (f32[1,32,256,128]{2,3,1,0:T(8,128)}, f32[1,32,256,128]{2,3,1,0:T(8,128)}, f32[1,32,256,128]{2,3,1,0:T(8,128)}, f32[1,32,256,128]{2,3,1,0:T(8,128)}) fusion(f32[2,32,256,128]{2,3,1,0:T(8,128)} %fusion.12, f32[2,32,256,128]{2,3,1,0:T(8,128)S(1)} %fusion.9, f32[1,32,256,128]{2,3,1,0:T(8,128)} %copy.106, f32[1,32,256,128]{2,3,1,0:T(8,128)S(1)} %copy-done.2), kind=kLoop, calls=%fused_computation.15 | loop fusion | flops 20971520 | bytes 41943040 | tf_op jit(solution)/shard_map/add | solution.py:103
  296.7 7.8 %maximum_bitcast_fusion = f32[2,32,256,128,1]{2,3,1,0,4:T(8,128)} fusion(f32[1,32,256,128]{2,3,1,0:T(8,128)} %get-tuple-element.20, f32[1,32,256,128]{2,3,1,0:T(8,128)} %get-tuple-element.21), kind=kLoop, calls=%fused_computation.2 | loop fusion | flops 2097152 | bytes 16777216 | tf_op jit(solution)/shard_map/stack | solution.py:97
  304.4 10.3 %copy.139 = f32[2,32,256,128,1]{3,1,0,2,4:T(8,128)} copy(f32[2,32,256,128,1]{2,3,1,0,4:T(8,128)} %maximum_bitcast_fusion) | data formatting | bytes 16777216 | tf_op jit(solution)/shard_map/stack | solution.py:97
  314.7 12.5 %convolution_bitcast_fusion = f32[2,32,256,128]{3,1,2,0:T(8,128)S(1)} fusion(f32[2,32,256,128,1]{3,1,0,2,4:T(8,128)} %copy.139, f32[1,2,128,128]{3,2,1,0:T(8,128)S(1)} %copy-done.11, f32[1,2,128,128]{3,2,1,0:T(8,128)S(1)} %copy-done.9), kind=kOutput, calls=%fused_computation.26 | convolution fusion | flops 6442516480 | bytes 17039360 | tf_op jit(solution)/shard_map/qzcn,pqkn->pzck/dot_general | solution.py:38
  333.6 5.3 %fusion.18 = (f32[16,128,256]{1,0,2:T(8,128)}, f32[16,128,256]{1,0,2:T(8,128)}, f32[16,128,256]{1,0,2:T(8,128)S(1)}) fusion(f32[2,16,256,128]{3,1,2,0:T(8,128)S(1)} %fusion.15, bf16[128,16,256]{0,2,1:T(8,128)(2,1)S(1)} %all-to-all-done.1, bf16[128,16,256]{0,2,1:T(8,128)(2,1)S(1)} %copy-done.4, bf16[128,16,256]{0,2,1:T(8,128)(2,1)} %all-to-all-done), kind=kLoop, calls=%fused_computation.33 | loop fusion | flops 3145728 | bytes 13631488 | tf_op jit(solution)/shard_map/mul | solution.py:144
  340.9 6.1 %all-to-all-start.4 = ((f32[16,128,256]{1,2,0:T(8,128)}), f32[16,128,256]{1,2,0:T(8,128)S(1)}, u32[]{:S(2)}, u32[]{:S(2)}) async-start(f32[16,128,256]{1,2,0:T(8,128)} %copy.120), calls=%async_computation.4 | async-start | bytes 4194304 | tf_op jit(solution)/shard_map/all_to_all | solution.py:135
  350.6 43.8 %all-to-all-done.4 = f32[16,128,256]{1,2,0:T(8,128)S(1)} async-done(((f32[16,128,256]{1,2,0:T(8,128)}), f32[16,128,256]{1,2,0:T(8,128)S(1)}, u32[]{:S(2)}, u32[]{:S(2)}) %all-to-all-start.4) | async-done | bytes 2097184 | tf_op jit(solution)/shard_map/all_to_all | solution.py:135
  403.0 43.9 %all-to-all-done.5 = f32[16,128,256]{1,2,0:T(8,128)} async-done(((f32[16,128,256]{1,2,0:T(8,128)}), f32[16,128,256]{1,2,0:T(8,128)}, u32[]{:S(2)}, u32[]{:S(2)}) %all-to-all-start.5) | async-done | bytes 2097184 | tf_op jit(solution)/shard_map/all_to_all | solution.py:136
  452.1 5.6 %copy.125 = f32[1,32,256,128]{3,2,1,0:T(8,128)} copy(f32[1,32,256,128]{2,3,1,0:T(8,128)} %get-tuple-element.19) | data formatting | bytes 8388608 | tf_op jit(solution)/shard_map/sub | solution.py:104
  460.7 5.6 %copy.123 = f32[1,32,256,128]{3,2,1,0:T(8,128)} copy(f32[1,32,256,128]{2,3,1,0:T(8,128)} %get-tuple-element.18) | data formatting | bytes 8388608 | tf_op jit(solution)/shard_map/add | solution.py:103
  475.9 23.6 %all-to-all-done.6 = f32[16,128,256]{1,2,0:T(8,128)} async-done(((f32[16,128,256]{1,2,0:T(8,128)}), f32[16,128,256]{1,2,0:T(8,128)}, u32[]{:S(2)}, u32[]{:S(2)}) %all-to-all-start.6) | async-done | bytes 2097184 | tf_op jit(solution)/shard_map/all_to_all | solution.py:143
  (99 shorter events, 78.2 us)
Async XLA Ops:
  7.2 179.2 %copy-start = (bf16[128,2048]{1,0:T(8,128)(2,1)S(1)}, bf16[128,2048]{1,0:T(8,128)(2,1)}, u32[]{:S(2)}) copy-start(bf16[128,2048]{1,0:T(8,128)(2,1)} %param.9) | copy-start | bytes 1572868
  7.2 9.7 %copy-start.13 = (bf16[128,4096]{1,0:T(8,128)(2,1)S(1)}, bf16[128,4096]{1,0:T(8,128)(2,1)}, u32[]{:S(2)}) copy-start(bf16[128,4096]{1,0:T(8,128)(2,1)} %param.8) | copy-start | bytes 3145732
  7.2 179.2 %all-gather.2.cloned.1.call-start = ((), (), s32[]{:S(2)}) async-start(), calls=%async_computation.7 | async-start | bytes 17825792 | tf_op jit(solution)/shard_map/all_gather | solution.py:121
  10.2 64.0 %copy-start.14 = (f32[16,2048]{1,0:T(8,128)S(1)}, f32[16,2048]{1,0:T(8,128)}, u32[]{:S(2)}) copy-start(f32[16,2048]{1,0:T(8,128)} %param.11) | copy-start | bytes 393220
  10.2 57.8 %all-to-all-start.1 = ((bf16[128,16,256]{0,2,1:T(8,128)(2,1)}), bf16[128,16,256]{0,2,1:T(8,128)(2,1)S(1)}, u32[]{:S(2)}, u32[]{:S(2)}) async-start(bf16[128,16,256]{0,2,1:T(8,128)(2,1)} %bitcast.30), calls=%async_computation.1 | async-start | bytes 2097152 | tf_op jit(solution)/shard_map/all_to_all | solution.py:126
  68.0 52.3 %all-to-all-start.2 = ((bf16[128,16,256]{0,2,1:T(8,128)(2,1)}), bf16[128,16,256]{0,2,1:T(8,128)(2,1)S(1)}, u32[]{:S(2)}, u32[]{:S(2)}) async-start(bf16[128,16,256]{0,2,1:T(8,128)(2,1)} %bitcast.224), calls=%async_computation.2 | async-start | bytes 2097152 | tf_op jit(solution)/shard_map/all_to_all | solution.py:127
  120.3 108.8 %copy-start.3 = (bf16[128,16,256]{0,2,1:T(8,128)(2,1)}, bf16[128,16,256]{0,2,1:T(8,128)(2,1)S(1)}, u32[]{:S(2)}) copy-start(bf16[128,16,256]{0,2,1:T(8,128)(2,1)S(1)} %all-to-all-done.2) | copy-start | bytes 3145732
  120.3 80.8 %all-to-all-start.3 = ((bf16[128,16,256]{0,2,1:T(8,128)(2,1)}), bf16[128,16,256]{0,2,1:T(8,128)(2,1)}, u32[]{:S(2)}, u32[]{:S(2)}) async-start(bf16[128,16,256]{0,2,1:T(8,128)(2,1)} %bitcast.223), calls=%async_computation.3 | async-start | bytes 2097152 | tf_op jit(solution)/shard_map/all_to_all | solution.py:125
  129.2 82.9 %copy-start.5 = (f32[1,2,128,128]{3,2,1,0:T(8,128)}, f32[1,2,128,128]{3,2,1,0:T(8,128)S(1)}, u32[]{:S(2)}) copy-start(f32[1,2,128,128]{3,2,1,0:T(8,128)S(1)} %get-tuple-element.38) | copy-start | bytes 393220
  129.2 82.9 %copy-start.7 = (f32[1,2,128,128]{3,2,1,0:T(8,128)}, f32[1,2,128,128]{3,2,1,0:T(8,128)S(1)}, u32[]{:S(2)}) copy-start(f32[1,2,128,128]{3,2,1,0:T(8,128)S(1)} %get-tuple-element.39) | copy-start | bytes 393220
  201.0 35.4 %all-to-all-start = ((bf16[128,16,256]{0,2,1:T(8,128)(2,1)}), bf16[128,16,256]{0,2,1:T(8,128)(2,1)}, u32[]{:S(2)}, u32[]{:S(2)}) async-start(bf16[128,16,256]{0,2,1:T(8,128)(2,1)} %bitcast.222), calls=%async_computation | async-start | bytes 2097152 | tf_op jit(solution)/shard_map/all_to_all | solution.py:128
  229.0 7.4 %copy-start.15 = (f32[1,16,32]{2,1,0:T(8,128)}, f32[1,16,32]{2,1,0:T(8,128)S(1)}, u32[]{:S(2)}) copy-start(f32[1,16,32]{2,1,0:T(8,128)S(1)} %get-tuple-element.43) | copy-start | bytes 6148
  229.1 7.4 %copy-start.17 = (f32[1,16,32]{2,1,0:T(8,128)}, f32[1,16,32]{2,1,0:T(8,128)S(1)}, u32[]{:S(2)}) copy-start(f32[1,16,32]{2,1,0:T(8,128)S(1)} %get-tuple-element.55) | copy-start | bytes 6148
  249.4 4.5 copy-start.6
  249.4 4.5 copy-start.8
  269.7 16.7 %copy-start.2 = (f32[1,32,256,128]{2,3,1,0:T(8,128)S(1)}, f32[1,32,256,128]{2,3,1,0:T(8,128)}, u32[]{:S(2)}) copy-start(f32[1,32,256,128]{2,3,1,0:T(8,128)} %copy.104) | copy-start | bytes 12582916
  304.4 10.3 %copy-start.9 = (f32[1,2,128,128]{3,2,1,0:T(8,128)S(1)}, f32[1,2,128,128]{3,2,1,0:T(8,128)}, u32[]{:S(2)}) copy-start(f32[1,2,128,128]{3,2,1,0:T(8,128)} %get-tuple-element.37) | copy-start | bytes 393220
  304.4 10.3 %copy-start.11 = (f32[1,2,128,128]{3,2,1,0:T(8,128)S(1)}, f32[1,2,128,128]{3,2,1,0:T(8,128)}, u32[]{:S(2)}) copy-start(f32[1,2,128,128]{3,2,1,0:T(8,128)} %get-tuple-element.40) | copy-start | bytes 393220
  328.6 5.0 copy-start.4
  340.9 53.5 %all-to-all-start.4 = ((f32[16,128,256]{1,2,0:T(8,128)}), f32[16,128,256]{1,2,0:T(8,128)S(1)}, u32[]{:S(2)}, u32[]{:S(2)}) async-start(f32[16,128,256]{1,2,0:T(8,128)} %copy.120), calls=%async_computation.4 | async-start | bytes 4194304 | tf_op jit(solution)/shard_map/all_to_all | solution.py:135
  394.4 52.4 %all-to-all-start.5 = ((f32[16,128,256]{1,2,0:T(8,128)}), f32[16,128,256]{1,2,0:T(8,128)}, u32[]{:S(2)}, u32[]{:S(2)}) async-start(f32[16,128,256]{1,2,0:T(8,128)} %copy.121), calls=%async_computation.5 | async-start | bytes 4194304 | tf_op jit(solution)/shard_map/all_to_all | solution.py:136
  446.8 52.7 %all-to-all-start.6 = ((f32[16,128,256]{1,2,0:T(8,128)}), f32[16,128,256]{1,2,0:T(8,128)}, u32[]{:S(2)}, u32[]{:S(2)}) async-start(f32[16,128,256]{1,2,0:T(8,128)} %copy.122), calls=%async_computation.6 | async-start | bytes 4194304 | tf_op jit(solution)/shard_map/all_to_all | solution.py:143
  466.3 3.8 copy-start.18
  473.0 29.4 %copy-start.1 = (bf16[128,2048]{1,0:T(8,128)(2,1)S(1)}, bf16[128,2048]{1,0:T(8,128)(2,1)}, u32[]{:S(2)}) copy-start(bf16[128,2048]{1,0:T(8,128)(2,1)} %param.9) | copy-start | bytes 1572868
  (5 other events, 16.9 us)
Sparse Core Ops, SparseCore 0:
  10.2 176.1 all-gather.1
where the time goes:
time: 516 us; the launch traced here: 510 us
  waiting for transfers between devices  265 us (51%)
  matrix products  70.3 us (14%)
  local copies, waits for them, and re-layouts  64.6 us (13%)
  other arithmetic  50.4 us (10%)
  starting transfers between devices  44.4 us (9%)
  between operations  14.9 us (3%)
    all_gather x1, waiting for transfers between devices, per_device(): lax.all_gather(out_weight, 'ctx', axis=0, tiled=True)  57.2 us
    all_to_all x1, waiting for transfers between devices, per_device(): lax.all_to_all(key_proj, 'ctx', split_axis=1, concat_axis=0, tiled=True)  49.8 us
    all_to_all x1, waiting for transfers between devices, per_device(): lax.all_to_all(value_proj, 'ctx', split_axis=1, concat_axis=0, tiled=True)  46.1 us
    all_to_all x1, waiting for transfers between devices, per_device(): lax.all_to_all(mixed_grad * value_cols.astype(jnp.float32), 'ctx', split_...  43.9 us
    all_to_all x1, waiting for transfers between devices, per_device(): lax.all_to_all(query_grad_cols, 'ctx', split_axis=0, concat_axis=1, tiled...  43.8 us
    dot_general x5, matrix products, apply_last(): jnp.einsum('qzcn,pqkn->pzck', spectrum, last_matrix(sign), precision=lax....  43 us
    all_to_all x1, waiting for transfers between devices, per_device(): lax.all_to_all(mixed_grad * key_cols.astype(jnp.float32), 'ctx', split_ax...  23.6 us
    mul x7, local copies, waits for them, and re-layouts, channel_work(): conv_real = filt_real * mix_real - filt_imag * mix_imag  16.2 us
  transfers between devices with their start and end apart: 8, of which 6 were waited for; matrix products, arithmetic and copies ran while one was open for 15% of the time, Pallas kernels for 0%

commit v1 on v0

--- a/solution.py
+++ b/solution.py
@@ -5,6 +5,19 @@
 from jax.sharding import PartitionSpec as P
 
 inner_len = 128
+
+
+def collect(array, axis, dim):
+    ways = lax.axis_size(axis)
+    up = [(d, (d + 1) % ways) for d in range(ways)]
+    down = [(d, (d - 1) % ways) for d in range(ways)]
+    earlier, later = ([array], [array])
+    for _ in range(ways // 2):
+        earlier.append(lax.ppermute(earlier[-1], axis, up))
+    for _ in range((ways - 1) // 2):
+        later.append(lax.ppermute(later[-1], axis, down))
+    line = jnp.concatenate([*earlier[::-1], *later[1:]], axis=dim)
+    return jnp.roll(line, (lax.axis_index(axis) - ways // 2) * array.shape[dim], axis=dim)
 
 
 def dft_pair(size_count):
@@ -116,10 +129,7 @@
 
 def per_device(query_proj, key_proj, value_proj, cotangent, out_weight, filters):
     grad_rows = jnp.einsum(
-        "tj,cj->tc",
-        cotangent,
-        lax.all_gather(out_weight, "ctx", axis=0, tiled=True),
-        preferred_element_type=jnp.float32,
+        "tj,cj->tc", cotangent, collect(out_weight, "ctx", 0), preferred_element_type=jnp.float32
     ).astype(jnp.bfloat16)
     query_cols, key_cols, value_cols, grad_cols = (
         lax.all_to_all(query_proj, "ctx", split_axis=1, concat_axis=0, tiled=True),

time: 516 us -> 582 us (1.13)
  starting transfers between devices: 44.4 us -> 167 us
  waiting for transfers between devices: 265 us -> 165 us
  local copies, waits for them, and re-layouts: 64.6 us -> 121 us
  between operations: 14.9 us -> 1.78 us
    ppermute x0 -> x15, starting transfers between devices: none -> 115 us  [the longest x7 106 us: collect(): later.append(lax.ppermute(later[-1], axis, down))]
    unnamed x54 -> x155, local copies, waits for them, and re-layouts: 15.3 us -> 72.7 us
    all_gather x1 -> x0, waiting for transfers between devices: 57.2 us -> none  [per_device(): lax.all_gather(out_weight, 'ctx', axis=0, tiled=True)]
    all_to_all x1, waiting for transfers between devices: 46.1 us -> 5.15 us  [per_device(): lax.all_to_all(value_proj, 'ctx', split_axis=1, concat_axis=0, tiled=True)]
    all_to_all x1, waiting for transfers between devices: 49.8 us -> 11 us  [per_device(): lax.all_to_all(key_proj, 'ctx', split_axis=1, concat_axis=0, tiled=True)]
    ppermute x0 -> x15, waiting for transfers between devices: none -> 37.8 us  [the longest x8 23.9 us: collect(): earlier.append(lax.ppermute(earlier[-1], axis, up))]
    all_to_all x1, starting transfers between devices: 7.06 us -> 19.8 us  [per_device(): lax.all_to_all(query_proj, 'ctx', split_axis=1, concat_axis=0, tiled=True)]
  transfers between devices with their start and end apart: 8 -> 22, of which waited for: 6 -> 13; matrix products, arithmetic and copies ran while one was open for 15% -> 23% of each run, Pallas kernels for 0% -> 0%
where the time goes in v1:
time: 582 us; the launch traced here: 573 us
  starting transfers between devices  167 us (29%)
  waiting for transfers between devices  165 us (28%)
  local copies, waits for them, and re-layouts  121 us (21%)
  matrix products  67.3 us (12%)
  other arithmetic  51 us (9%)
    ppermute x7, starting transfers between devices, collect(): later.append(lax.ppermute(later[-1], axis, down))  106 us
    unnamed x155, local copies, waits for them, and re-layouts  72.7 us
    all_to_all x1, waiting for transfers between devices, per_device(): lax.all_to_all(mixed_grad * value_cols.astype(jnp.float32), 'ctx', split_...  43.9 us
    all_to_all x1, waiting for transfers between devices, per_device(): lax.all_to_all(query_grad_cols, 'ctx', split_axis=0, concat_axis=1, tiled...  43.8 us
    dot_general x5, matrix products, apply_last(): jnp.einsum('qzcn,pqkn->pzck', spectrum, last_matrix(sign), precision=lax....  43.1 us
    ppermute x8, waiting for transfers between devices, collect(): earlier.append(lax.ppermute(earlier[-1], axis, up))  23.9 us
    all_to_all x1, waiting for transfers between devices, per_device(): lax.all_to_all(mixed_grad * key_cols.astype(jnp.float32), 'ctx', split_ax...  23.5 us
    all_to_all x1, starting transfers between devices, per_device(): lax.all_to_all(query_proj, 'ctx', split_axis=1, concat_axis=0, tiled=True)  19.8 us
  transfers between devices with their start and end apart: 22, of which 13 were waited for; matrix products, arithmetic and copies ran while one was open for 23% of the time, Pallas kernels for 0%

profile of v1, /device:TPU:13, one launch (start us, length us, event | category | flops | bytes accessed | tf_op | source)
XLA Modules:
  0.0 573.0 jit_solution(5439214471979146351)
XLA Ops:
  2.5 12.1 %collective-permute-done = bf16[256,2048]{1,0:T(8,128)(2,1)S(1)} collective-permute-done((bf16[256,2048]{1,0:T(8,128)(2,1)}, bf16[256,2048]{1,0:T(8,128)(2,1)S(1)}, u32[]{:S(2)}, u32[]{:S(2)}) %collective-permute-start) | collective-permute-done | bytes 1048608 | tf_op jit(solution)/shard_map/ppermute | solution.py:16
  17.9 11.8 %collective-permute-done.1 = bf16[256,2048]{1,0:T(8,128)(2,1)S(1)} collective-permute-done((bf16[256,2048]{1,0:T(8,128)(2,1)S(1)}, bf16[256,2048]{1,0:T(8,128)(2,1)S(1)}, u32[]{:S(2)}, u32[]{:S(2)}) %collective-permute-start.1) | collective-permute-done | bytes 1048608 | tf_op jit(solution)/shard_map/ppermute | solution.py:16
  34.3 19.2 %collective-permute-start.9 = (bf16[256,2048]{1,0:T(8,128)(2,1)S(1)}, bf16[256,2048]{1,0:T(8,128)(2,1)S(1)}, u32[]{:S(2)}, u32[]{:S(2)}) collective-permute-start(bf16[256,2048]{1,0:T(8,128)(2,1)S(1)} %collective-permute-done.8), channel_id=1, source_target_pairs={{0,15},{1,0},{2,1},{3,2},{4,3},{5,4},{6,5},{7,6},{8,7},{9,8},{10,9... | collective-permute-start | bytes 3145736 | tf_op jit(solution)/shard_map/ppermute | solution.py:18
  55.7 21.2 %collective-permute-start.10 = (bf16[256,2048]{1,0:T(8,128)(2,1)S(1)}, bf16[256,2048]{1,0:T(8,128)(2,1)S(1)}, u32[]{:S(2)}, u32[]{:S(2)}) collective-permute-start(bf16[256,2048]{1,0:T(8,128)(2,1)S(1)} %collective-permute-done.9), channel_id=1, source_target_pairs={{0,15},{1,0},{2,1},{3,2},{4,3},{5,4},{6,5},{7,6},{8,7},{9,8},{10,9... | collective-permute-start | bytes 3145736 | tf_op jit(solution)/shard_map/ppermute | solution.py:18
  80.7 22.7 %collective-permute-start.11 = (bf16[256,2048]{1,0:T(8,128)(2,1)S(1)}, bf16[256,2048]{1,0:T(8,128)(2,1)S(1)}, u32[]{:S(2)}, u32[]{:S(2)}) collective-permute-start(bf16[256,2048]{1,0:T(8,128)(2,1)S(1)} %collective-permute-done.10), channel_id=1, source_target_pairs={{0,15},{1,0},{2,1},{3,2},{4,3},{5,4},{6,5},{7,6},{8,7},{9,8},{10,9... | collective-permute-start | bytes 3145736 | tf_op jit(solution)/shard_map/ppermute | solution.py:18
  105.6 21.8 %collective-permute-start.12 = (bf16[256,2048]{1,0:T(8,128)(2,1)S(1)}, bf16[256,2048]{1,0:T(8,128)(2,1)}, u32[]{:S(2)}, u32[]{:S(2)}) collective-permute-start(bf16[256,2048]{1,0:T(8,128)(2,1)S(1)} %collective-permute-done.11), channel_id=1, source_target_pairs={{0,15},{1,0},{2,1},{3,2},{4,3},{5,4},{6,5},{7,6},{8,7},{9,8},{10,9... | collective-permute-start | bytes 3145736 | tf_op jit(solution)/shard_map/ppermute | solution.py:18
  129.8 20.9 %collective-permute-start.13 = (bf16[256,2048]{1,0:T(8,128)(2,1)}, bf16[256,2048]{1,0:T(8,128)(2,1)}, u32[]{:S(2)}, u32[]{:S(2)}) collective-permute-start(bf16[256,2048]{1,0:T(8,128)(2,1)} %collective-permute-done.12), channel_id=1, source_target_pairs={{0,15},{1,0},{2,1},{3,2},{4,3},{5,4},{6,5},{7,6},{8,7},{9,8},{10,9... | collective-permute-start | bytes 3145736 | tf_op jit(solution)/shard_map/ppermute | solution.py:18
  153.1 19.8 %all-to-all-start.3 = ((bf16[128,16,256]{0,2,1:T(8,128)(2,1)}), bf16[128,16,256]{0,2,1:T(8,128)(2,1)S(1)}, u32[]{:S(2)}, u32[]{:S(2)}) async-start(bf16[128,16,256]{0,2,1:T(8,128)(2,1)} %bitcast.224), calls=%async_computation.3 | async-start | bytes 2097152 | tf_op jit(solution)/shard_map/all_to_all | solution.py:135
  215.8 5.7 all-to-all-start.1
  235.3 11.0 %all-to-all-done.1 = bf16[128,16,256]{0,2,1:T(8,128)(2,1)S(1)} async-done(((bf16[128,16,256]{0,2,1:T(8,128)(2,1)}), bf16[128,16,256]{0,2,1:T(8,128)(2,1)S(1)}, u32[]{:S(2)}, u32[]{:S(2)}) %all-to-all-start.1) | async-done | bytes 1048608 | tf_op jit(solution)/shard_map/all_to_all | solution.py:136
  261.7 9.2 %fusion.11 = bf16[4096,128]{1,0:T(8,128)(2,1)} fusion(bf16[128,2048]{1,0:T(8,128)(2,1)S(1)} %copy-done, bf16[8192,2048]{1,0:T(8,128)(2,1)} %constant_dynamic-update-slice_fusion, s32[]{:T(128)S(6)} %select_n.152), kind=kOutput, calls=%fused_computation.15 | convolution fusion | flops 2148007936 | bytes 18350084 | tf_op jit(solution)/shard_map/tj,cj->tc/dot_general | solution.py:131
  285.3 5.6 copy.102
  301.0 5.7 fusion.31
  313.1 6.3 %multiply_subtract_fusion.3 = (f32[1,32,256,128]{3,1,2,0:T(8,128)}, f32[1,32,256,128]{3,1,2,0:T(8,128)}, f32[1,32,256,128]{3,1,2,0:T(8,128)S(1)}, f32[1,32,256,128]{3,1,2,0:T(8,128)}) fusion(f32[2,32,256,128]{3,1,2,0:T(8,128)S(1)} %bitcast.213, f32[32,128]{1,0:T(8,128)S(1)} %copy-done.42, f32[32,128]{1,0:T(8,128)S(1)} %get-tuple-element.50, ...), kind=kLoop, calls=%fused_computation.25 | loop fusion | flops 12582912 | bytes 33587200 | tf_op jit(solution)/shard_map/sub | solution.py:39
  323.9 12.6 %fusion.14 = f32[2,32,256,128]{2,3,1,0:T(8,128)S(1)} fusion(f32[2,32,256,128]{3,1,2,0:T(8,128)S(1)} %pad_maximum_fusion, f32[1,2,128,128]{3,2,1,0:T(8,128)S(1)} %copy-done.33, f32[1,2,128,128]{3,2,1,0:T(8,128)S(1)} %copy-done.35), kind=kOutput, calls=%fused_computation.26 | convolution fusion | flops 6442516480 | bytes 17039360 | tf_op jit(solution)/shard_map/qzcn,pqkn->pzck/dot_general | solution.py:51
  339.7 16.8 %fusion.17 = f32[2,32,256,128]{2,3,1,0:T(8,128)} fusion(f32[2,32,256,128]{3,1,2,0:T(8,128)S(1)} %pad_maximum_fusion.1, f32[1,2,128,128]{3,2,1,0:T(8,128)S(1)} %copy-done.33, f32[1,2,128,128]{3,2,1,0:T(8,128)S(1)} %copy-done.35), kind=kOutput, calls=%fused_computation.27 | convolution fusion | flops 6442516480 | bytes 17039360 | tf_op jit(solution)/shard_map/qzcn,pqkn->pzck/dot_general | solution.py:51
  356.5 10.3 %multiply_add_fusion = (f32[1,32,256,128]{2,3,1,0:T(8,128)}, f32[1,32,256,128]{2,3,1,0:T(8,128)}, f32[1,32,256,128]{2,3,1,0:T(8,128)}, f32[1,32,256,128]{2,3,1,0:T(8,128)}) fusion(f32[2,32,256,128]{2,3,1,0:T(8,128)} %fusion.17, f32[2,32,256,128]{2,3,1,0:T(8,128)S(1)} %fusion.14, f32[1,32,256,128]{2,3,1,0:T(8,128)} %copy.104, f32[1,32,256,128]{2,3,1,0:T(8,128)S(1)} %copy-done.2), kind=kLoop, calls=%fused_computation.17 | loop fusion | flops 20971520 | bytes 41943040 | tf_op jit(solution)/shard_map/add | solution.py:116
  366.8 7.8 %maximum_bitcast_fusion = f32[2,32,256,128,1]{2,3,1,0,4:T(8,128)} fusion(f32[1,32,256,128]{2,3,1,0:T(8,128)} %get-tuple-element.20, f32[1,32,256,128]{2,3,1,0:T(8,128)} %get-tuple-element.21), kind=kLoop, calls=%fused_computation.4 | loop fusion | flops 2097152 | bytes 16777216 | tf_op jit(solution)/shard_map/stack | solution.py:110
  374.6 10.4 %copy.137 = f32[2,32,256,128,1]{3,1,0,2,4:T(8,128)} copy(f32[2,32,256,128,1]{2,3,1,0,4:T(8,128)} %maximum_bitcast_fusion) | data formatting | bytes 16777216 | tf_op jit(solution)/shard_map/stack | solution.py:110
  385.0 12.5 %convolution_bitcast_fusion = f32[2,32,256,128]{3,1,2,0:T(8,128)S(1)} fusion(f32[2,32,256,128,1]{3,1,0,2,4:T(8,128)} %copy.137, f32[1,2,128,128]{3,2,1,0:T(8,128)S(1)} %copy-done.38, f32[1,2,128,128]{3,2,1,0:T(8,128)S(1)} %copy-done.36), kind=kOutput, calls=%fused_computation.28 | convolution fusion | flops 6442516480 | bytes 17039360 | tf_op jit(solution)/shard_map/qzcn,pqkn->pzck/dot_general | solution.py:51
  411.2 6.0 %all-to-all-start.4 = ((f32[16,128,256]{1,2,0:T(8,128)}), f32[16,128,256]{1,2,0:T(8,128)S(1)}, u32[]{:S(2)}, u32[]{:S(2)}) async-start(f32[16,128,256]{1,2,0:T(8,128)} %copy.118), calls=%async_computation.4 | async-start | bytes 4194304 | tf_op jit(solution)/shard_map/all_to_all | solution.py:145
  420.8 43.8 %all-to-all-done.4 = f32[16,128,256]{1,2,0:T(8,128)S(1)} async-done(((f32[16,128,256]{1,2,0:T(8,128)}), f32[16,128,256]{1,2,0:T(8,128)S(1)}, u32[]{:S(2)}, u32[]{:S(2)}) %all-to-all-start.4) | async-done | bytes 2097184 | tf_op jit(solution)/shard_map/all_to_all | solution.py:145
  473.2 43.9 %all-to-all-done.5 = f32[16,128,256]{1,2,0:T(8,128)} async-done(((f32[16,128,256]{1,2,0:T(8,128)}), f32[16,128,256]{1,2,0:T(8,128)}, u32[]{:S(2)}, u32[]{:S(2)}) %all-to-all-start.5) | async-done | bytes 2097184 | tf_op jit(solution)/shard_map/all_to_all | solution.py:146
  546.2 23.5 %all-to-all-done.6 = f32[16,128,256]{1,2,0:T(8,128)} async-done(((f32[16,128,256]{1,2,0:T(8,128)}), f32[16,128,256]{1,2,0:T(8,128)}, u32[]{:S(2)}, u32[]{:S(2)}) %all-to-all-start.6) | async-done | bytes 2097184 | tf_op jit(solution)/shard_map/all_to_all | solution.py:153
  (227 shorter events, 190.8 us)
Async XLA Ops:
  0.6 261.1 %copy-start = (bf16[128,2048]{1,0:T(8,128)(2,1)S(1)}, bf16[128,2048]{1,0:T(8,128)(2,1)}, u32[]{:S(2)}) copy-start(bf16[128,2048]{1,0:T(8,128)(2,1)} %param.9) | copy-start | bytes 1572868
  0.7 13.9 %collective-permute-start = (bf16[256,2048]{1,0:T(8,128)(2,1)}, bf16[256,2048]{1,0:T(8,128)(2,1)S(1)}, u32[]{:S(2)}, u32[]{:S(2)}) collective-permute-start(bf16[256,2048]{1,0:T(8,128)(2,1)} %param.10), channel_id=1, source_target_pairs={{0,1},{1,2},{2,3},{3,4},{4,5},{5,6},{6,7},{7,8},{8,9},{9,10},{10,1... | collective-permute-start | bytes 3145736 | tf_op jit(solution)/shard_map/ppermute | solution.py:16
  14.6 179.2 %copy-start.9 = (bf16[256,2048]{1,0:T(8,128)(2,1)}, bf16[256,2048]{1,0:T(8,128)(2,1)S(1)}, u32[]{:S(2)}) copy-start(bf16[256,2048]{1,0:T(8,128)(2,1)S(1)} %collective-permute-done) | copy-start | bytes 3145732
  14.6 15.1 %collective-permute-start.1 = (bf16[256,2048]{1,0:T(8,128)(2,1)S(1)}, bf16[256,2048]{1,0:T(8,128)(2,1)S(1)}, u32[]{:S(2)}, u32[]{:S(2)}) collective-permute-start(bf16[256,2048]{1,0:T(8,128)(2,1)S(1)} %collective-permute-done), channel_id=1, source_target_pairs={{0,1},{1,2},{2,3},{3,4},{4,5},{5,6},{6,7},{7,8},{8,9},{9,10},{10,1... | collective-permute-start | bytes 3145736 | tf_op jit(solution)/shard_map/ppermute | solution.py:16
  17.8 15.4 %collective-permute-start.8 = (bf16[256,2048]{1,0:T(8,128)(2,1)}, bf16[256,2048]{1,0:T(8,128)(2,1)S(1)}, u32[]{:S(2)}, u32[]{:S(2)}) collective-permute-start(bf16[256,2048]{1,0:T(8,128)(2,1)} %param.10), channel_id=1, source_target_pairs={{0,15},{1,0},{2,1},{3,2},{4,3},{5,4},{6,5},{7,6},{8,7},{9,8},{10,9... | collective-permute-start | bytes 3145736 | tf_op jit(solution)/shard_map/ppermute | solution.py:18
  29.6 23.8 %collective-permute-start.2 = (bf16[256,2048]{1,0:T(8,128)(2,1)S(1)}, bf16[256,2048]{1,0:T(8,128)(2,1)S(1)}, u32[]{:S(2)}, u32[]{:S(2)}) collective-permute-start(bf16[256,2048]{1,0:T(8,128)(2,1)S(1)} %collective-permute-done.1), channel_id=1, source_target_pairs={{0,1},{1,2},{2,3},{3,4},{4,5},{5,6},{6,7},{7,8},{8,9},{9,10},{10,1... | collective-permute-start | bytes 3145736 | tf_op jit(solution)/shard_map/ppermute | solution.py:16
  34.3 21.4 %collective-permute-start.9 = (bf16[256,2048]{1,0:T(8,128)(2,1)S(1)}, bf16[256,2048]{1,0:T(8,128)(2,1)S(1)}, u32[]{:S(2)}, u32[]{:S(2)}) collective-permute-start(bf16[256,2048]{1,0:T(8,128)(2,1)S(1)} %collective-permute-done.8), channel_id=1, source_target_pairs={{0,15},{1,0},{2,1},{3,2},{4,3},{5,4},{6,5},{7,6},{8,7},{9,8},{10,9... | collective-permute-start | bytes 3145736 | tf_op jit(solution)/shard_map/ppermute | solution.py:18
  53.4 23.5 %collective-permute-start.3 = (bf16[256,2048]{1,0:T(8,128)(2,1)S(1)}, bf16[256,2048]{1,0:T(8,128)(2,1)S(1)}, u32[]{:S(2)}, u32[]{:S(2)}) collective-permute-start(bf16[256,2048]{1,0:T(8,128)(2,1)S(1)} %collective-permute-done.2), channel_id=1, source_target_pairs={{0,1},{1,2},{2,3},{3,4},{4,5},{5,6},{6,7},{7,8},{8,9},{9,10},{10,1... | collective-permute-start | bytes 3145736 | tf_op jit(solution)/shard_map/ppermute | solution.py:16
  55.7 24.0 %collective-permute-start.10 = (bf16[256,2048]{1,0:T(8,128)(2,1)S(1)}, bf16[256,2048]{1,0:T(8,128)(2,1)S(1)}, u32[]{:S(2)}, u32[]{:S(2)}) collective-permute-start(bf16[256,2048]{1,0:T(8,128)(2,1)S(1)} %collective-permute-done.9), channel_id=1, source_target_pairs={{0,15},{1,0},{2,1},{3,2},{4,3},{5,4},{6,5},{7,6},{8,7},{9,8},{10,9... | collective-permute-start | bytes 3145736 | tf_op jit(solution)/shard_map/ppermute | solution.py:18
  76.9 26.4 %collective-permute-start.4 = (bf16[256,2048]{1,0:T(8,128)(2,1)S(1)}, bf16[256,2048]{1,0:T(8,128)(2,1)S(1)}, u32[]{:S(2)}, u32[]{:S(2)}) collective-permute-start(bf16[256,2048]{1,0:T(8,128)(2,1)S(1)} %collective-permute-done.3), channel_id=1, source_target_pairs={{0,1},{1,2},{2,3},{3,4},{4,5},{5,6},{6,7},{7,8},{8,9},{9,10},{10,1... | collective-permute-start | bytes 3145736 | tf_op jit(solution)/shard_map/ppermute | solution.py:16
  80.7 24.9 %collective-permute-start.11 = (bf16[256,2048]{1,0:T(8,128)(2,1)S(1)}, bf16[256,2048]{1,0:T(8,128)(2,1)S(1)}, u32[]{:S(2)}, u32[]{:S(2)}) collective-permute-start(bf16[256,2048]{1,0:T(8,128)(2,1)S(1)} %collective-permute-done.10), channel_id=1, source_target_pairs={{0,15},{1,0},{2,1},{3,2},{4,3},{5,4},{6,5},{7,6},{8,7},{9,8},{10,9... | collective-permute-start | bytes 3145736 | tf_op jit(solution)/shard_map/ppermute | solution.py:18
  103.3 24.1 %collective-permute-start.5 = (bf16[256,2048]{1,0:T(8,128)(2,1)S(1)}, bf16[256,2048]{1,0:T(8,128)(2,1)S(1)}, u32[]{:S(2)}, u32[]{:S(2)}) collective-permute-start(bf16[256,2048]{1,0:T(8,128)(2,1)S(1)} %collective-permute-done.4), channel_id=1, source_target_pairs={{0,1},{1,2},{2,3},{3,4},{4,5},{5,6},{6,7},{7,8},{8,9},{9,10},{10,1... | collective-permute-start | bytes 3145736 | tf_op jit(solution)/shard_map/ppermute | solution.py:16
  105.6 24.2 %collective-permute-start.12 = (bf16[256,2048]{1,0:T(8,128)(2,1)S(1)}, bf16[256,2048]{1,0:T(8,128)(2,1)}, u32[]{:S(2)}, u32[]{:S(2)}) collective-permute-start(bf16[256,2048]{1,0:T(8,128)(2,1)S(1)} %collective-permute-done.11), channel_id=1, source_target_pairs={{0,15},{1,0},{2,1},{3,2},{4,3},{5,4},{6,5},{7,6},{8,7},{9,8},{10,9... | collective-permute-start | bytes 3145736 | tf_op jit(solution)/shard_map/ppermute | solution.py:18
  127.4 23.3 %collective-permute-start.6 = (bf16[256,2048]{1,0:T(8,128)(2,1)S(1)}, bf16[256,2048]{1,0:T(8,128)(2,1)}, u32[]{:S(2)}, u32[]{:S(2)}) collective-permute-start(bf16[256,2048]{1,0:T(8,128)(2,1)S(1)} %collective-permute-done.5), channel_id=1, source_target_pairs={{0,1},{1,2},{2,3},{3,4},{4,5},{5,6},{6,7},{7,8},{8,9},{9,10},{10,1... | collective-permute-start | bytes 3145736 | tf_op jit(solution)/shard_map/ppermute | solution.py:16
  129.8 50.7 %collective-permute-start.13 = (bf16[256,2048]{1,0:T(8,128)(2,1)}, bf16[256,2048]{1,0:T(8,128)(2,1)}, u32[]{:S(2)}, u32[]{:S(2)}) collective-permute-start(bf16[256,2048]{1,0:T(8,128)(2,1)} %collective-permute-done.12), channel_id=1, source_target_pairs={{0,15},{1,0},{2,1},{3,2},{4,3},{5,4},{6,5},{7,6},{8,7},{9,8},{10,9... | collective-permute-start | bytes 3145736 | tf_op jit(solution)/shard_map/ppermute | solution.py:18
  150.8 30.2 %collective-permute-start.7 = (bf16[256,2048]{1,0:T(8,128)(2,1)}, bf16[256,2048]{1,0:T(8,128)(2,1)}, u32[]{:S(2)}, u32[]{:S(2)}) collective-permute-start(bf16[256,2048]{1,0:T(8,128)(2,1)} %collective-permute-done.6), channel_id=1, source_target_pairs={{0,1},{1,2},{2,3},{3,4},{4,5},{5,6},{6,7},{7,8},{8,9},{9,10},{10,1... | collective-permute-start | bytes 3145736 | tf_op jit(solution)/shard_map/ppermute | solution.py:16
  153.1 62.7 %all-to-all-start.3 = ((bf16[128,16,256]{0,2,1:T(8,128)(2,1)}), bf16[128,16,256]{0,2,1:T(8,128)(2,1)S(1)}, u32[]{:S(2)}, u32[]{:S(2)}) async-start(bf16[128,16,256]{0,2,1:T(8,128)(2,1)} %bitcast.224), calls=%async_computation.3 | async-start | bytes 2097152 | tf_op jit(solution)/shard_map/all_to_all | solution.py:135
  180.6 28.4 %collective-permute-start.14 = (bf16[256,2048]{1,0:T(8,128)(2,1)}, bf16[256,2048]{1,0:T(8,128)(2,1)S(1)}, u32[]{:S(2)}, u32[]{:S(2)}) collective-permute-start(bf16[256,2048]{1,0:T(8,128)(2,1)} %collective-permute-done.13), channel_id=1, source_target_pairs={{0,15},{1,0},{2,1},{3,2},{4,3},{5,4},{6,5},{7,6},{8,7},{9,8},{10,9... | collective-permute-start | bytes 3145736 | tf_op jit(solution)/shard_map/ppermute | solution.py:18
  215.8 30.5 %all-to-all-start.1 = ((bf16[128,16,256]{0,2,1:T(8,128)(2,1)}), bf16[128,16,256]{0,2,1:T(8,128)(2,1)S(1)}, u32[]{:S(2)}, u32[]{:S(2)}) async-start(bf16[128,16,256]{0,2,1:T(8,128)(2,1)} %bitcast.225), calls=%async_computation.1 | async-start | bytes 2097152 | tf_op jit(solution)/shard_map/all_to_all | solution.py:136
  246.3 29.8 %all-to-all-start.2 = ((bf16[128,16,256]{0,2,1:T(8,128)(2,1)}), bf16[128,16,256]{0,2,1:T(8,128)(2,1)S(1)}, u32[]{:S(2)}, u32[]{:S(2)}) async-start(bf16[128,16,256]{0,2,1:T(8,128)(2,1)} %bitcast.223), calls=%async_computation.2 | async-start | bytes 2097152 | tf_op jit(solution)/shard_map/all_to_all | solution.py:137
  276.1 30.5 %all-to-all-start = ((bf16[128,16,256]{0,2,1:T(8,128)(2,1)}), bf16[128,16,256]{0,2,1:T(8,128)(2,1)}, u32[]{:S(2)}, u32[]{:S(2)}) async-start(bf16[128,16,256]{0,2,1:T(8,128)(2,1)} %bitcast.228), calls=%async_computation | async-start | bytes 2097152 | tf_op jit(solution)/shard_map/all_to_all | solution.py:138
  411.2 53.4 %all-to-all-start.4 = ((f32[16,128,256]{1,2,0:T(8,128)}), f32[16,128,256]{1,2,0:T(8,128)S(1)}, u32[]{:S(2)}, u32[]{:S(2)}) async-start(f32[16,128,256]{1,2,0:T(8,128)} %copy.118), calls=%async_computation.4 | async-start | bytes 4194304 | tf_op jit(solution)/shard_map/all_to_all | solution.py:145
  464.6 52.4 %all-to-all-start.5 = ((f32[16,128,256]{1,2,0:T(8,128)}), f32[16,128,256]{1,2,0:T(8,128)}, u32[]{:S(2)}, u32[]{:S(2)}) async-start(f32[16,128,256]{1,2,0:T(8,128)} %copy.119), calls=%async_computation.5 | async-start | bytes 4194304 | tf_op jit(solution)/shard_map/all_to_all | solution.py:146
  517.0 52.7 %all-to-all-start.6 = ((f32[16,128,256]{1,2,0:T(8,128)}), f32[16,128,256]{1,2,0:T(8,128)}, u32[]{:S(2)}, u32[]{:S(2)}) async-start(f32[16,128,256]{1,2,0:T(8,128)} %copy.120), calls=%async_computation.6 | async-start | bytes 4194304 | tf_op jit(solution)/shard_map/all_to_all | solution.py:153
  (54 other events, 1039.8 us)
